TPU v7x, 32 devices: a whole 2x2x4 slice. The times are simulated.
32 devices in a mesh: ctx: 8 (over z, x), head: 4 (over y, core).
Axes of the slice: x: 2, y: 2, z: 4, core: 2. Of those that a mesh axis runs over, the one named last changes fastest.
Arguments:
- keys: bfloat16 [16384, 5120], P('ctx', 'head'), may hold values from -6 to 6
- values: bfloat16 [16384, 5120], P('ctx', 'head'), may hold values from -6 to 6
- queries: bfloat16 [16384, 5120], P('ctx', 'head'), may hold values from -6 to 6
- rates: float32 [16384, 16], P('ctx', 'head'), may hold values from 9.765625e-05 to 0.0009765625
- w_gate: bfloat16 [320, 16, 320], P('ctx', 'head'), may hold values from -0.3125 to 0.3125
- w_up: bfloat16 [320, 16, 320], P('ctx', 'head'), may hold values from -0.3125 to 0.3125
- w_down: bfloat16 [320, 16, 320], P('ctx', 'head'), may hold values from -0.3125 to 0.3125
- gain: float32 [5120], P('head'), may hold values from 0.5 to 1.5
Outputs:
- output: bfloat16 [16384, 5120], P('ctx', 'head')
- new_gate: bfloat16 [320, 16, 320], P('ctx', 'head')
- new_up: bfloat16 [320, 16, 320], P('ctx', 'head')
- new_down: bfloat16 [320, 16, 320], P('ctx', 'head')
All inputs are finite; a program needn't handle non-finite values.
Results may differ from a plain program's by a relative error of at most 0.0092.
Values may be sent and summed in bfloat16 or wider, within the bound.
A program may use at most 128 MiB of HBM per device.

v0:
```python
import jax
import jax.numpy as jnp
from jax import lax
from jax.sharding import PartitionSpec as P

HEADS = 16
DH = 320
EPS = 1e-06


def per_device(keys, values, queries, rates, w_gate, w_up, w_down, gain):
    rows = keys.shape[0]
    heads = w_gate.shape[1]
    width = w_gate.shape[2]
    local_units = w_gate.shape[0]
    keyh = keys.reshape(rows, heads, width)
    valueh = values.reshape(rows, heads, width)
    queryh = queries.reshape(rows, heads, width)
    full_gate, full_up, full_down = (
        lax.all_gather(w_gate, "ctx", axis=0, tiled=True),
        lax.all_gather(w_up, "ctx", axis=0, tiled=True),
        lax.all_gather(w_down, "ctx", axis=0, tiled=True),
    )
    gpre = jnp.einsum("thd,fhd->thf", keyh, full_gate, preferred_element_type=jnp.float32)
    upre = jnp.einsum("thd,fhd->thf", keyh, full_up, preferred_element_type=jnp.float32)
    sig = jax.nn.sigmoid(gpre)
    act = gpre * sig
    slope = sig * (1.0 + gpre * (1.0 - sig))
    hidden = (act * upre).astype(jnp.bfloat16)
    scaled = (valueh.astype(jnp.float32) * rates[:, :, None]).astype(jnp.bfloat16)
    back = jnp.einsum("thd,fhd->thf", scaled, full_down, preferred_element_type=jnp.float32)
    dgate = (back * upre * slope).astype(jnp.bfloat16)
    dup = (back * act).astype(jnp.bfloat16)
    grad_gate = jnp.einsum("thf,thd->fhd", dgate, keyh, preferred_element_type=jnp.float32)
    grad_up = jnp.einsum("thf,thd->fhd", dup, keyh, preferred_element_type=jnp.float32)
    grad_down = jnp.einsum("thf,thd->fhd", hidden, scaled, preferred_element_type=jnp.float32)
    total = lax.psum(jnp.stack([grad_gate, grad_up, grad_down], axis=1), "ctx")
    olds = jnp.stack([full_gate, full_up, full_down], axis=1).astype(jnp.float32)
    updated = olds + total
    old_sq = jnp.sum(olds * olds, axis=0)
    new_sq = jnp.sum(updated * updated, axis=0)
    fresh = (updated * (jnp.sqrt(old_sq) * lax.rsqrt(new_sq + EPS))[None]).astype(jnp.bfloat16)
    offset = lax.axis_index("ctx") * local_units
    mine = lax.dynamic_slice_in_dim(fresh, offset, local_units, 0)
    new_gate = fresh[:, 0]
    new_up = fresh[:, 1]
    new_down = fresh[:, 2]
    qgate = jnp.einsum("thd,fhd->thf", queryh, new_gate, preferred_element_type=jnp.float32)
    qup = jnp.einsum("thd,fhd->thf", queryh, new_up, preferred_element_type=jnp.float32)
    mixed = (jax.nn.silu(qgate) * qup).astype(jnp.bfloat16)
    outh = jnp.einsum("thf,fhd->thd", mixed, new_down, preferred_element_type=jnp.float32)
    squares = lax.psum(jnp.sum(outh * outh, axis=(1, 2)), "head")
    scale = lax.rsqrt(squares / (HEADS * DH) + EPS)
    result = outh * scale[:, None, None] * gain.reshape(heads, width)[None]
    output = result.reshape(rows, heads * width).astype(jnp.bfloat16)
    return (output, mine[:, 0], mine[:, 1], mine[:, 2])


def solution(mesh):
    in_specs = (
        P("ctx", "head"),
        P("ctx", "head"),
        P("ctx", "head"),
        P("ctx", "head"),
        P("ctx", "head", None),
        P("ctx", "head", None),
        P("ctx", "head", None),
        P("head"),
    )
    out_specs = (
        P("ctx", "head"),
        P("ctx", "head", None),
        P("ctx", "head", None),
        P("ctx", "head", None),
    )
    return jax.shard_map(
        per_device, mesh=mesh, in_specs=in_specs, out_specs=out_specs, check_vma=False
    )
```

profile of v0, /device:TPU:0, one launch (start us, length us, event | category | flops | bytes accessed | tf_op | source)
XLA Modules:
  0.0 447.1 jit_solution(6353832946601583923)
XLA Ops:
  7.2 0.0 copy-start.5
  7.2 0.0 copy-start.6
  7.2 0.0 all-reduce.2.cloned.1.call-start
  7.2 7.9 %copy.31 = bf16[2048,1280]{0,1:T(8,128)(2,1)} copy(bf16[2048,1280]{1,0:T(8,128)(2,1)} %param.8) | data formatting | bytes 10485760 | tf_op args[0]
  15.2 0.0 copy-done.5
  15.2 34.4 %all_gather.9 = bf16[320,4,320]{2,0,1:T(8,128)(2,1)S(1)} all-gather(bf16[40,4,320]{2,0,1:T(8,128)(2,1)S(1)} %copy.27), channel_id=1, replica_groups=mesh['ctx'=8,'head'=4] {'ctx'}, dimensions={0}, use_global_device_ids=true | all-gather | bytes 921600 | tf_op jit(solution)/shard_map/all_gather | solution.py:20
  49.6 0.0 copy-done.6
  49.7 0.0 slice-start
  49.7 32.8 %all_gather.10 = bf16[320,4,320]{2,0,1:T(8,128)(2,1)S(1)} all-gather(bf16[40,4,320]{2,0,1:T(8,128)(2,1)S(1)} %copy.28), channel_id=1, replica_groups=mesh['ctx'=8,'head'=4] {'ctx'}, dimensions={0}, use_global_device_ids=true | all-gather | bytes 921600 | tf_op jit(solution)/shard_map/all_gather | solution.py:21
  82.4 0.0 slice-start.1
  82.4 8.1 %fusion.45 = f32[4,320,2048]{2,1,0:T(8,128)} fusion(bf16[320,4,320]{2,0,1:T(8,128)(2,1)S(1)} %all_gather.9, bf16[2048,4,320]{0,2,1:T(8,128)(2,1)} %bitcast.133), kind=kOutput, calls=%fused_computation.56 | convolution fusion | flops 1677721600 | bytes 16547840 | tf_op jit(solution)/shard_map/thd,fhd->thf/dot_general | solution.py:24
  90.5 0.0 slice-done
  90.5 0.0 slice-done.1
  90.5 5.4 %fusion.44 = f32[4,320,2048]{2,1,0:T(8,128)} fusion(bf16[320,4,320]{2,0,1:T(8,128)(2,1)S(1)} %all_gather.10, bf16[2048,4,320]{0,2,1:T(8,128)(2,1)S(1)} %bitcast.138), kind=kOutput, calls=%fused_computation.55 | convolution fusion | flops 1677721600 | bytes 16547840 | tf_op jit(solution)/shard_map/thd,fhd->thf/dot_general | solution.py:25
  95.9 0.0 copy-start.7
  95.9 8.0 %copy.30 = bf16[2048,1280]{0,1:T(8,128)(2,1)} copy(bf16[2048,1280]{1,0:T(8,128)(2,1)} %param.9) | data formatting | bytes 10485760 | tf_op args[1]
  103.9 0.0 copy-done.7
  103.9 33.2 %all_gather.11 = bf16[320,4,320]{2,0,1:T(8,128)(2,1)S(1)} all-gather(bf16[40,4,320]{2,0,1:T(8,128)(2,1)S(1)} %copy.29), channel_id=1, replica_groups=mesh['ctx'=8,'head'=4] {'ctx'}, dimensions={0}, use_global_device_ids=true | all-gather | bytes 921600 | tf_op jit(solution)/shard_map/all_gather | solution.py:22
  137.1 0.0 copy-done.4
  137.1 7.9 %fusion.24 = f32[4,2048,320]{1,2,0:T(8,128)} fusion(bf16[320,4,320]{2,0,1:T(8,128)(2,1)S(1)} %all_gather.11, bf16[2048,4,320]{0,2,1:T(8,128)(2,1)} %bitcast.143, f32[2048,4]{0,1:T(4,128)S(1)} %copy-done.4), kind=kOutput, calls=%fused_computation.36 | convolution fusion | flops 1685585920 | bytes 16580608 | tf_op jit(solution)/shard_map/thd,fhd->thf/dot_general | solution.py:31
  145.0 13.0 %fusion.31 = f32[320,1,4,320]{3,0,2,1:T(8,128)} fusion(f32[4,320,2048]{2,1,0:T(8,128)} %fusion.44, f32[4,320,2048]{2,1,0:T(8,128)} %fusion.45, bf16[2048,4,320]{0,2,1:T(8,128)(2,1)} %bitcast.144, f32[2048,4]{0,1:T(4,128)S(1)} %copy-done.4), kind=kOutput, calls=%fused_computation.40 | convolution fusion | flops 1701314560 | bytes 27885568 | tf_op jit(solution)/shard_map/thf,thd->fhd/dot_general | solution.py:36
  158.1 15.3 %fusion.28 = f32[320,1,4,320]{3,0,2,1:T(8,128)} fusion(bf16[2048,4,320]{0,2,1:T(8,128)(2,1)} %bitcast.134, f32[4,320,2048]{2,1,0:T(8,128)} %fusion.45, f32[4,320,2048]{2,1,0:T(8,128)} %fusion.44, f32[4,2048,320]{1,2,0:T(8,128)} %fusion.24), kind=kOutput, calls=%fused_computation.39 | convolution fusion | flops 1703936000 | bytes 38338560 | tf_op jit(solution)/shard_map/thf,thd->fhd/dot_general | solution.py:34
  173.3 10.7 %fusion.36 = f32[320,1,4,320]{3,0,2,1:T(8,128)S(1)} fusion(bf16[2048,4,320]{0,2,1:T(8,128)(2,1)} %bitcast.135, f32[4,2048,320]{1,2,0:T(8,128)} %fusion.24, f32[4,320,2048]{2,1,0:T(8,128)} %fusion.45), kind=kOutput, calls=%fused_computation.41 | convolution fusion | flops 1693450240 | bytes 27852800 | tf_op jit(solution)/shard_map/thf,thd->fhd/dot_general | solution.py:35
  184.1 0.0 copy-done.2
  184.1 0.0 copy-done.3
  184.1 3.0 pad_maximum_fusion
  187.1 0.0 all-reduce.2.cloned.1.call-update
  187.1 0.0 copy-start.8
  187.1 8.1 %copy.33 = bf16[2048,1280]{0,1:T(8,128)(2,1)} copy(bf16[2048,1280]{1,0:T(8,128)(2,1)} %param.10) | data formatting | bytes 10485760 | tf_op args[2]
  195.3 0.0 copy-done.8
  195.3 0.1 mul.103
  195.3 194.0 %all-reduce.2.cloned.1.call-done = f32[320,3,4,320]{3,0,2,1:T(8,128)} async-done(((f32[320,3,4,320]{3,0,2,1:T(8,128)}), f32[320,3,4,320]{3,0,2,1:T(8,128)}) %all-reduce.2.cloned.1.call-update) | async-done | bytes 4915216 | tf_op jit(solution)/shard_map/psum | solution.py:37
  389.4 3.6 fusion.14
  393.0 0.8 copy-done
  393.8 1.0 multiply_convert_fusion.1
  394.8 0.0 copy-start.1
  394.8 1.6 copy-done.1
  396.4 0.0 slice-done.2
  396.4 0.0 slice-done.3
  396.4 5.4 %fusion.39 = f32[4,320,2048]{2,1,0:T(8,128)} fusion(bf16[2048,4,320]{0,2,1:T(8,128)(2,1)S(1)} %bitcast.142, bf16[320,3,4,320]{3,0,2,1:T(8,128)(2,1)S(1)} %multiply_convert_fusion.1), kind=kOutput, calls=%fused_computation.44 | convolution fusion | flops 1677721600 | bytes 16711680 | tf_op jit(solution)/shard_map/thd,fhd->thf/dot_general | solution.py:48
  401.8 13.7 %multiply_reduce_fusion = (f32[2048]{0:T(1024)S(1)}, f32[4,320,2048]{2,1,0:T(8,128)}) fusion(f32[4,320,2048]{2,1,0:T(8,128)} %fusion.39, bf16[2048,4,320]{0,2,1:T(8,128)(2,1)} %bitcast.139, bf16[320,3,4,320]{3,0,2,1:T(8,128)(2,1)} %copy-done.1), kind=kOutput, calls=%fused_computation.25 | convolution fusion | flops 3376412672 | bytes 28188672 | tf_op jit(solution)/shard_map/thf,fhd->thd/dot_general | solution.py:51
  415.5 6.5 %psum.15 = f32[2048]{0:T(1024)S(1)} all-reduce(f32[2048]{0:T(1024)S(1)} %get-tuple-element.17), channel_id=1, replica_groups=mesh['ctx'=8,'head'=4] {'head'}, use_global_device_ids=true, to_apply=%region_4.5 | all-reduce | flops 2048 | bytes 16384 | tf_op jit(solution)/shard_map/psum | solution.py:52
  422.0 7.3 %multiply_convert_fusion = bf16[4,320,2048]{2,1,0:T(8,128)(2,1)} fusion(f32[4,320,2048]{2,1,0:T(8,128)} %get-tuple-element.18, f32[4,320]{1,0:T(4,128)S(1)} %mul.103, f32[2048]{0:T(1024)S(1)} %add_rsqrt_fusion), kind=kLoop, calls=%fused_computation.24 | loop fusion | flops 7864320 | bytes 15741952 | tf_op jit(solution)/shard_map/convert_element_type | solution.py:55
  429.3 7.9 %copy.35 = bf16[2048,1280]{1,0:T(8,128)(2,1)} copy(bf16[2048,1280]{0,1:T(8,128)(2,1)} %bitcast.145) | data formatting | bytes 10485760
  437.2 1.1 dynamic-slice_bitcast_fusion
  438.2 0.7 copy.36
  438.9 0.7 copy.37
  439.6 0.7 copy.38
  (13 shorter events, 0.1 us)
Async XLA Ops:
  7.2 8.0 %copy-start.5 = (bf16[40,4,320]{2,1,0:T(4,128)(2,1)S(1)}, bf16[40,4,320]{2,1,0:T(4,128)(2,1)}, u32[]{:S(2)}) copy-start(bf16[40,4,320]{2,1,0:T(4,128)(2,1)} %param.12) | copy-start | bytes 307204
  7.2 42.5 %copy-start.6 = (bf16[40,4,320]{2,1,0:T(4,128)(2,1)S(1)}, bf16[40,4,320]{2,1,0:T(4,128)(2,1)}, u32[]{:S(2)}) copy-start(bf16[40,4,320]{2,1,0:T(4,128)(2,1)} %param.13) | copy-start | bytes 307204
  7.2 382.2 %all-reduce.2.cloned.1.call-start = ((), (), s32[]{:S(2)}) async-start(), calls=%async_computation | async-start | bytes 11796480 | tf_op jit(solution)/shard_map/psum | solution.py:37
  49.7 40.9 %slice-start = ((s8[5242880]{0:T(1024)(128)(4,1)}), s8[4194304]{0:T(1024)(128)(4,1)S(1)}, s32[]{:S(2)}) async-start(s8[5242880]{0:T(1024)(128)(4,1)} %bitcast.136), calls=%async_computation.1 | async-start | bytes 8388608
  82.4 8.1 %slice-start.1 = ((s8[5242880]{0:T(1024)(128)(4,1)}), s8[1048576]{0:T(1024)(128)(4,1)S(1)}, s32[]{:S(2)}) async-start(s8[5242880]{0:T(1024)(128)(4,1)} %bitcast.136), calls=%async_computation.2 | async-start | bytes 2097152
  95.9 8.0 %copy-start.7 = (bf16[40,4,320]{2,1,0:T(4,128)(2,1)S(1)}, bf16[40,4,320]{2,1,0:T(4,128)(2,1)}, u32[]{:S(2)}) copy-start(bf16[40,4,320]{2,1,0:T(4,128)(2,1)} %param.14) | copy-start | bytes 307204
  95.9 41.2 %copy-start.4 = (f32[2048,4]{0,1:T(4,128)S(1)}, f32[2048,4]{0,1:T(4,128)}, u32[]{:S(2)}) copy-start(f32[2048,4]{0,1:T(4,128)} %param.11) | copy-start | bytes 98308
  173.3 10.7 %copy-start.2 = (f32[320,1,4,320]{3,0,2,1:T(8,128)S(1)}, f32[320,1,4,320]{3,0,2,1:T(8,128)}, u32[]{:S(2)}) copy-start(f32[320,1,4,320]{3,0,2,1:T(8,128)} %fusion.31) | copy-start | bytes 4915204
  173.3 10.7 %copy-start.3 = (f32[320,1,4,320]{3,0,2,1:T(8,128)S(1)}, f32[320,1,4,320]{3,0,2,1:T(8,128)}, u32[]{:S(2)}) copy-start(f32[320,1,4,320]{3,0,2,1:T(8,128)} %fusion.28) | copy-start | bytes 4915204
  187.1 8.2 %copy-start.8 = (f32[1280]{0:T(1024)S(1)}, f32[1280]{0:T(1024)}, u32[]{:S(2)}) copy-start(f32[1280]{0:T(1024)} %param.15) | copy-start | bytes 15364
  389.4 4.4 copy-start
  389.4 7.0 %slice-start.2 = ((s8[5242880]{0:T(1024)(128)(4,1)}), s8[4194304]{0:T(1024)(128)(4,1)S(1)}, s32[]{:S(2)}) async-start(s8[5242880]{0:T(1024)(128)(4,1)} %bitcast.140), calls=%async_computation.3 | async-start | bytes 8388608
  393.8 2.6 slice-start.3
  394.8 1.6 copy-start.1
Sparse Core Ops, SparseCore 0:
  187.2 202.0 all-reduce.1
where the time goes:
time: 448 us; the launch traced here: 447 us
  waiting for transfers between devices  194 us (43%)
  blocking collectives  107 us (24%)
  matrix products  79.5 us (18%)
  local copies, waits for them, and re-layouts  37.6 us (8%)
  other arithmetic  14.9 us (3%)
  between operations  14.2 us (3%)
    psum x1, waiting for transfers between devices, per_device(): total = lax.psum(jnp.stack([grad_gate, grad_up, grad_down], axis=1), 'ctx')  194 us
    unnamed x36, local copies, waits for them, and re-layouts  36.5 us
    all_gather x1, blocking collectives, per_device(): lax.all_gather(w_gate, 'ctx', axis=0, tiled=True)  34.4 us
    all_gather x1, blocking collectives, per_device(): lax.all_gather(w_down, 'ctx', axis=0, tiled=True)  33.2 us
    all_gather x1, blocking collectives, per_device(): lax.all_gather(w_up, 'ctx', axis=0, tiled=True)  32.8 us
    dot_general x1, matrix products, per_device(): jnp.einsum('thf,thd->fhd', dgate, keyh, preferred_element_type=jnp.float32)  15.3 us
    dot_general x1, matrix products, per_device(): jnp.einsum('thf,fhd->thd', mixed, new_down, preferred_element_type=jnp.fl...  13.7 us
    dot_general x1, matrix products, per_device(): jnp.einsum('thf,thd->fhd', hidden, scaled, preferred_element_type=jnp.flo...  13 us
  transfers between devices with their start and end apart: 1, of which 1 were waited for; matrix products, arithmetic and copies ran while one was open for 2% of the time, Pallas kernels for 0%

commit v1 on v0

--- a/solution.py
+++ b/solution.py
@@ -34,7 +34,9 @@
     grad_gate = jnp.einsum("thf,thd->fhd", dgate, keyh, preferred_element_type=jnp.float32)
     grad_up = jnp.einsum("thf,thd->fhd", dup, keyh, preferred_element_type=jnp.float32)
     grad_down = jnp.einsum("thf,thd->fhd", hidden, scaled, preferred_element_type=jnp.float32)
-    total = lax.psum(jnp.stack([grad_gate, grad_up, grad_down], axis=1), "ctx")
+    x = jnp.stack([grad_gate, grad_up, grad_down], axis=1)
+    parts = lax.all_gather(x, "ctx")
+    total = jnp.sum(parts, axis=0)
     olds = jnp.stack([full_gate, full_up, full_down], axis=1).astype(jnp.float32)
     updated = olds + total
     old_sq = jnp.sum(olds * olds, axis=0)

time: 448 us -> 1160 us (2.59)
  waiting for transfers between devices: 194 us -> 886 us
  other arithmetic: 14.9 us -> 34.1 us
    all_gather x0 -> x1, waiting for transfers between devices: none -> 886 us  [per_device(): parts = lax.all_gather(x, 'ctx')]
    psum x1 -> x0, waiting for transfers between devices: 194 us -> none  [per_device(): total = lax.psum(jnp.stack([grad_gate, grad_up, grad_down], axis=1), 'ctx')]
    reduce_sum x0 -> x1, other arithmetic: none -> 19.3 us  [per_device(): total = jnp.sum(parts, axis=0)]
  transfers between devices with their start and end apart: 1 -> 1, of which waited for: 1 -> 1; matrix products, arithmetic and copies ran while one was open for 2% -> 1% of each run, Pallas kernels for 0% -> 0%
where the time goes in v1:
time: 1160 us
  waiting for transfers between devices  886 us (76%)
  blocking collectives  107 us (9%)
  matrix products  79.5 us (7%)
  local copies, waits for them, and re-layouts  37.4 us (3%)
  other arithmetic  34.1 us (3%)
  between operations  14.2 us (1%)
    all_gather x1, waiting for transfers between devices, per_device(): parts = lax.all_gather(x, 'ctx')  886 us
    unnamed x36, local copies, waits for them, and re-layouts  36.2 us
    all_gather x1, blocking collectives, per_device(): lax.all_gather(w_gate, 'ctx', axis=0, tiled=True)  34.4 us
    all_gather x1, blocking collectives, per_device(): lax.all_gather(w_down, 'ctx', axis=0, tiled=True)  33 us
    all_gather x1, blocking collectives, per_device(): lax.all_gather(w_up, 'ctx', axis=0, tiled=True)  32.8 us
  transfers between devices with their start and end apart: 1, of which 1 were waited for; matrix products, arithmetic and copies ran while one was open for 1% of the time, Pallas kernels for 0%

profile of v1, /device:TPU:0, one launch (start us, length us, event | category | flops | bytes accessed | tf_op | source)
XLA Modules:
  0.0 1158.2 jit_solution(9646375408305158142)
XLA Ops:
  7.2 0.0 copy-start.5
  7.2 0.0 copy-start.6
  7.2 0.0 all-gather.3.cloned.1.call-start
  7.2 7.9 copy.31
  15.2 0.0 copy-done.5
  15.2 34.4 %all_gather.15 = bf16[320,4,320]{2,0,1:T(8,128)(2,1)S(1)} all-gather(bf16[40,4,320]{2,0,1:T(8,128)(2,1)S(1)} %copy.27), channel_id=1, replica_groups=mesh['ctx'=8,'head'=4] {'ctx'}, dimensions={0}, use_global_device_ids=true | all-gather | bytes 921600 | tf_op jit(solution)/shard_map/all_gather | solution.py:20
  49.6 0.0 copy-done.6
  49.7 0.0 slice-start
  49.7 32.8 %all_gather.16 = bf16[320,4,320]{2,0,1:T(8,128)(2,1)S(1)} all-gather(bf16[40,4,320]{2,0,1:T(8,128)(2,1)S(1)} %copy.28), channel_id=1, replica_groups=mesh['ctx'=8,'head'=4] {'ctx'}, dimensions={0}, use_global_device_ids=true | all-gather | bytes 921600 | tf_op jit(solution)/shard_map/all_gather | solution.py:21
  82.4 0.0 slice-start.1
  82.4 8.1 fusion.45
  90.5 0.0 slice-done
  90.5 0.0 slice-done.1
  90.5 5.4 fusion.44
  95.9 8.0 copy.30
  103.9 0.0 copy-done.7
  103.9 33.0 %all_gather.17 = bf16[320,4,320]{2,0,1:T(8,128)(2,1)S(1)} all-gather(bf16[40,4,320]{2,0,1:T(8,128)(2,1)S(1)} %copy.29), channel_id=1, replica_groups=mesh['ctx'=8,'head'=4] {'ctx'}, dimensions={0}, use_global_device_ids=true | all-gather | bytes 921600 | tf_op jit(solution)/shard_map/all_gather | solution.py:22
  136.9 0.0 copy-done.4
  136.9 7.9 fusion.24
  144.8 13.0 %fusion.31 = f32[320,1,4,320]{3,0,2,1:T(8,128)} fusion(f32[4,320,2048]{2,1,0:T(8,128)} %fusion.44, f32[4,320,2048]{2,1,0:T(8,128)} %fusion.45, bf16[2048,4,320]{0,2,1:T(8,128)(2,1)} %bitcast.146, f32[2048,4]{0,1:T(4,128)S(1)} %copy-done.4), kind=kOutput, calls=%fused_computation.40 | convolution fusion | flops 1701314560 | bytes 27885568 | tf_op jit(solution)/shard_map/thf,thd->fhd/dot_general | solution.py:36
  157.9 15.3 %fusion.28 = f32[320,1,4,320]{3,0,2,1:T(8,128)} fusion(bf16[2048,4,320]{0,2,1:T(8,128)(2,1)} %bitcast.135, f32[4,320,2048]{2,1,0:T(8,128)} %fusion.45, f32[4,320,2048]{2,1,0:T(8,128)} %fusion.44, f32[4,2048,320]{1,2,0:T(8,128)} %fusion.24), kind=kOutput, calls=%fused_computation.39 | convolution fusion | flops 1703936000 | bytes 38338560 | tf_op jit(solution)/shard_map/thf,thd->fhd/dot_general | solution.py:34
  173.2 10.7 fusion.36
  183.9 0.0 copy-done.2
  183.9 0.0 copy-done.3
  183.9 2.9 pad_maximum_fusion
  186.8 0.0 all-gather.3.cloned.1.call-update
  186.8 0.0 copy-start.8
  186.8 7.9 copy.33
  194.7 0.0 copy-done.8
  194.7 0.1 mul.103
  194.8 886.3 %all-gather.3.cloned.1.call-done = f32[2560,3,4,320]{3,0,2,1:T(8,128)} async-done(((f32[320,3,4,320]{3,0,2,1:T(8,128)}), f32[2560,3,4,320]{3,0,2,1:T(8,128)}) %all-gather.3.cloned.1.call-update) | async-done | bytes 39321616 | tf_op jit(solution)/shard_map/all_gather | solution.py:38
  1081.1 19.3 %reduce_sum.36 = f32[320,3,4,320]{3,0,2,1:T(8,128)} reduce(f32[8,320,3,4,320]{4,1,0,3,2:T(8,128)} %bitcast.140, f32[]{:T(128)} %constant.10.clone.1), dimensions={0}, to_apply=%region_0.0 | reduce | flops 8601600 | bytes 44236804 | tf_op jit(solution)/shard_map/reduce_sum | solution.py:39
  1100.4 3.6 fusion.14
  1104.0 0.8 copy-done
  1104.8 1.0 multiply_convert_fusion.1
  1105.8 0.0 copy-start.1
  1105.9 1.6 copy-done.1
  1107.5 0.0 slice-done.2
  1107.5 0.0 slice-done.3
  1107.5 5.4 fusion.39
  1112.8 13.7 %multiply_reduce_fusion = (f32[2048]{0:T(1024)S(1)}, f32[4,320,2048]{2,1,0:T(8,128)}) fusion(f32[4,320,2048]{2,1,0:T(8,128)} %fusion.39, bf16[2048,4,320]{0,2,1:T(8,128)(2,1)} %bitcast.141, bf16[320,3,4,320]{3,0,2,1:T(8,128)(2,1)} %copy-done.1), kind=kOutput, calls=%fused_computation.25 | convolution fusion | flops 3376412672 | bytes 28188672 | tf_op jit(solution)/shard_map/thf,fhd->thd/dot_general | solution.py:53
  1126.6 6.5 psum.7
  1133.1 7.3 multiply_convert_fusion
  1140.3 7.9 copy.35
  1148.2 1.1 dynamic-slice_bitcast_fusion
  1149.3 0.7 copy.36
  1150.0 0.7 copy.37
  1150.6 0.7 copy.38
  (14 shorter events, 0.1 us)
Async XLA Ops:
  7.2 8.0 copy-start.5
  7.2 42.5 %copy-start.6 = (bf16[40,4,320]{2,1,0:T(4,128)(2,1)S(1)}, bf16[40,4,320]{2,1,0:T(4,128)(2,1)}, u32[]{:S(2)}) copy-start(bf16[40,4,320]{2,1,0:T(4,128)(2,1)} %param.13) | copy-start | bytes 307204
  7.2 1073.9 %all-gather.3.cloned.1.call-start = ((), (), s32[]{:S(2)}) async-start(), calls=%async_computation | async-start | bytes 53084160 | tf_op jit(solution)/shard_map/all_gather | solution.py:38
  49.7 40.9 %slice-start = ((s8[5242880]{0:T(1024)(128)(4,1)}), s8[4194304]{0:T(1024)(128)(4,1)S(1)}, s32[]{:S(2)}) async-start(s8[5242880]{0:T(1024)(128)(4,1)} %bitcast.137), calls=%async_computation.1 | async-start | bytes 8388608
  82.4 8.1 slice-start.1
  95.9 8.0 copy-start.7
  95.9 41.0 %copy-start.4 = (f32[2048,4]{0,1:T(4,128)S(1)}, f32[2048,4]{0,1:T(4,128)}, u32[]{:S(2)}) copy-start(f32[2048,4]{0,1:T(4,128)} %param.11) | copy-start | bytes 98308
  173.2 10.7 copy-start.2
  173.2 10.7 copy-start.3
  186.8 7.9 copy-start.8
  1100.4 4.4 copy-start
  1100.4 7.0 slice-start.2
  1104.8 2.6 slice-start.3
  1105.8 1.6 copy-start.1
Sparse Core Ops, SparseCore 0:
  186.9 894.0 all-gather.2
